TPU v7x, 128 devices: a whole 4x4x4 slice. The times are simulated.
128 devices in a mesh: leaf: 16 (over x_lo, y, core), grid: 8 (over x_hi, z).
Axes of the slice: x: 4 (x_hi: 2, x_lo: 2; x = x_hi * 2 + x_lo), y: 4, z: 4, core: 2. Of those that a mesh axis runs over, the one named last changes fastest.
Arguments:
- child_front: float32 [16, 1, 2048, 2, 8, 128], P('leaf', None, None, None, 'grid'), as said below
- child_live: int32 [16, 1, 16], replicated, may hold values 0 or 1
- child_map: int32 [16, 1, 8], replicated, may hold values from 0 to 15, as said below
- parent_owner: int32 [8, 16], replicated, may hold values from 0 to 15, as said below
- parent_shift: float32 [16, 1, 1, 8, 128], P('leaf', None, None, 'grid'), may hold values from 0.5 to 2
Outputs:
- child_factor: float32 [16, 1, 2048, 1, 8, 128], P('leaf', None, None, None, 'grid')
- parent_done: float32 [16, 1, 2048, 1, 8, 128], P('leaf', None, None, None, 'grid')
Inputs may be any that keep to these rules, and one draw needn't show every extreme that they name: `child_map`: each row holds 8 different block numbers in increasing order, the last one being 15. `parent_owner`: each row is a permutation of the 16 slots. `child_front`: each front is symmetric positive definite.
All inputs are finite; a program needn't handle non-finite values.
Results may differ from a plain program's by a relative error of at most 0.0003.
Values sent between devices are 32-bit elements; how exact they have to be, the bound alone decides.
No kernel may reach another device: no remote copies, remote signals or barrier semaphores. Data moves between devices by JAX's collectives and lax.ppermute only.
A program may use at most 128 MiB of HBM per device.

v0:
```python
import jax
import jax.numpy as jnp
from jax import lax
from jax.sharding import PartitionSpec as P

F = 2048
PIVOTS = 1024
NB = 128
CORDER = 1024
FB = 16
PB = 8
CB = 8
highest = lax.Precision.HIGHEST


def broadcast(value, axis, root):
    mine = lax.axis_index(axis) == root
    return lax.psum(jnp.where(mine, value, jnp.zeros_like(value)), axis)


def swapped_2(value, axis, distance):
    mask = 2**distance
    pairs = [(source, source ^ mask) for source in range(lax.axis_size(axis))]
    return lax.ppermute(value, axis, pairs)


def panel_factor(column_tail):
    lower_part = jnp.linalg.cholesky(column_tail[:, :NB])
    below_part = lax.linalg.triangular_solve(
        lower_part, column_tail[:, NB:], left_side=False, lower=True, transpose_a=True
    )
    return jnp.concatenate([lower_part, below_part], axis=1)


def apply_panel(front_cols, panel_cols, block_ids, panel):
    first_row = panel * NB
    pieces = []
    for round_pick in range(front_cols.shape[2]):
        target = block_ids[round_pick]
        offset = jnp.clip(target * NB - first_row, 0, F - first_row - NB)
        partner = lax.dynamic_slice_in_dim(panel_cols, offset, NB, 1)
        change = jnp.einsum("frn,fsn->frs", panel_cols, partner, precision=highest)
        current = front_cols[:, first_row:, round_pick, :]
        updated = jnp.where(target > panel, current - change, current)
        updated = jnp.where(target == panel, panel_cols, updated)
        upper_rows = jnp.where(target == panel, 0.0, front_cols[:, :first_row, round_pick, :])
        pieces.append(jnp.concatenate([upper_rows, updated], axis=1))
    return jnp.stack(pieces, axis=2)


def mask_front(front_cols, alive_mask, block_ids):
    live_rows = jnp.repeat(alive_mask, NB, axis=1)
    choose = (jnp.arange(FB)[:, None] == block_ids[None, :]).astype(jnp.float32)
    live_cols = jnp.dot(alive_mask, choose, precision=highest)
    places = block_ids[:, None] * NB + jnp.arange(NB)[None, :]
    diagonal = (jnp.arange(F)[:, None, None] == places[None]).astype(jnp.float32)
    kept = front_cols * live_rows[:, :, None, None] * live_cols[:, None, :, None]
    return kept + diagonal[None] * (1.0 - live_cols)[:, None, :, None]


def place_column(schur, targets, alive_mask, target):
    fronts = schur.shape[0]
    pick = (targets == target).astype(jnp.float32) * alive_mask
    tiles = schur.reshape(fronts, CORDER, CB, NB)
    column = jnp.einsum("fc,frcj->frj", pick, tiles, precision=highest)
    spread = (targets[:, None, :] == jnp.arange(FB)[None, :, None]).astype(
        jnp.float32
    ) * alive_mask[:, None, :]
    placed = jnp.einsum(
        "fbc,fcij->fbij", spread, column.reshape(fronts, CB, NB, NB), precision=highest
    )
    return placed.reshape(fronts, F, NB)


def body(child_front, child_live, child_map, parent_owner, parent_shift):
    grid_count = lax.axis_size("grid")
    grid_pos = lax.axis_index("grid")
    leaf_pos = lax.axis_index("leaf")
    member = leaf_pos % 2
    pair = leaf_pos // 2
    sibling = leaf_pos ^ 1
    fronts = child_front.shape[1]
    child_rounds = child_front.shape[3]
    pivot_rounds = PIVOTS // (NB * grid_count)
    parent_rounds = parent_shift.shape[2]
    my_alive = lax.dynamic_index_in_dim(child_live, leaf_pos, 0, keepdims=False).astype(jnp.float32)
    other_alive = lax.dynamic_index_in_dim(child_live, sibling, 0, keepdims=False).astype(
        jnp.float32
    )
    my_map = lax.dynamic_index_in_dim(child_map, leaf_pos, 0, keepdims=False)
    other_map = lax.dynamic_index_in_dim(child_map, sibling, 0, keepdims=False)
    child_blocks = jnp.arange(child_rounds) * grid_count + grid_pos
    front_cols = mask_front(
        child_front.reshape(fronts, F, child_rounds, NB), my_alive, child_blocks
    )
    for panel in range(PB):
        column = front_cols[:, :, panel // grid_count, :]
        outgoing = column
        arrived = broadcast(outgoing, "grid", panel % grid_count)
        column_tail = arrived[:, panel * NB :]
        front_cols = apply_panel(front_cols, panel_factor(column_tail), child_blocks, panel)
    child_factor = front_cols[:, :, :pivot_rounds, :]
    contrib = front_cols[:, PIVOTS:, pivot_rounds:, :]
    gathered = lax.all_gather(contrib[:, :, :, None, :], "grid", axis=3, tiled=True)
    mine_schur = gathered.reshape(fronts, CORDER, CORDER)
    other_schur = swapped_2(mine_schur, "leaf", 0)
    owner_row = lax.dynamic_index_in_dim(parent_owner, pair, 0, keepdims=False)
    slot_ids = (member * grid_count + grid_pos) * parent_rounds + jnp.arange(parent_rounds)
    holders = (owner_row[:, None] == slot_ids[None, :]).astype(jnp.int32)
    parent_blocks = jnp.sum(holders * jnp.arange(FB)[:, None], axis=0)
    shift_cols = parent_shift.reshape(fronts, parent_rounds, NB)
    my_live_contrib = my_alive[:, PB:]
    other_live_contrib = other_alive[:, PB:]
    target = parent_blocks[0]
    column = place_column(mine_schur, my_map, my_live_contrib, target)
    column = column + place_column(other_schur, other_map, other_live_contrib, target)
    places = target * NB + jnp.arange(NB)
    diagonal = (jnp.arange(F)[:, None] == places[None, :]).astype(jnp.float32)
    pieces = [column + diagonal[None] * shift_cols[:, 0, None, :]]
    parent_cols = jnp.stack(pieces, axis=2)
    for panel in range(PB):
        holder = owner_row[panel]
        holder_side = holder // (grid_count * parent_rounds)
        holder_grid = holder // parent_rounds % grid_count
        holder_round = holder % parent_rounds
        column = lax.dynamic_index_in_dim(parent_cols, holder_round, 2, keepdims=False)
        outgoing = column
        arrived = broadcast(outgoing, "grid", holder_grid)
        swapped = swapped_2(arrived, "leaf", 0)
        received = jnp.where(member == holder_side, arrived, swapped)
        column_tail = received[:, panel * NB :]
        parent_cols = apply_panel(parent_cols, panel_factor(column_tail), parent_blocks, panel)
    upper_part = (jnp.arange(F) < PIVOTS)[None, :, None, None] & (parent_blocks >= PB)[
        None, None, :, None
    ]
    parent_cols = jnp.where(upper_part, 0.0, parent_cols)
    return (
        child_factor.reshape(1, fronts, F, pivot_rounds, 1, NB),
        parent_cols.reshape(1, fronts, F, parent_rounds, 1, NB),
    )


def solution(mesh):
    in_specs = (
        P("leaf", None, None, None, "grid", None),
        P(),
        P(),
        P(),
        P("leaf", None, None, "grid", None),
    )
    out_specs = (
        P("leaf", None, None, None, "grid", None),
        P("leaf", None, None, None, "grid", None),
    )
    return jax.shard_map(body, mesh=mesh, in_specs=in_specs, out_specs=out_specs, check_vma=False)
```

profile of v0, /device:TPU:1, one launch (start us, length us, event | category | flops | bytes accessed | tf_op | source)
XLA Modules:
  0.0 2009.4 jit_solution(2481067446718470726)
XLA Ops:
  19.1 83.7 %all-reduce.17.cloned.1.call-done = f32[1,2048,128]{1,2,0:T(8,128)} async-done(((f32[1,2048,128]{1,2,0:T(8,128)}), f32[1,2048,128]{1,2,0:T(8,128)}) %all-reduce.17.cloned.1.call-update) | async-done | bytes 1048592 | tf_op jit(solution)/shard_map/psum | solution.py:18
  104.7 11.7 custom-call.50
  135.0 84.5 %all-reduce.19.cloned.1.call-done = f32[1,2048,128]{1,2,0:T(8,128)} async-done(((f32[1,2048,128]{1,2,0:T(8,128)}), f32[1,2048,128]{1,2,0:T(8,128)}) %all-reduce.19.cloned.1.call-update) | async-done | bytes 1048592 | tf_op jit(solution)/shard_map/psum | solution.py:18
  221.3 11.7 custom-call.52
  250.7 84.3 %all-reduce.21.cloned.1.call-done = f32[1,2048,128]{1,2,0:T(8,128)} async-done(((f32[1,2048,128]{1,2,0:T(8,128)}), f32[1,2048,128]{1,2,0:T(8,128)}) %all-reduce.21.cloned.1.call-update) | async-done | bytes 1048592 | tf_op jit(solution)/shard_map/psum | solution.py:18
  336.7 11.7 custom-call.54
  386.0 64.7 %all-reduce.23.cloned.1.call-done = f32[1,2048,128]{1,2,0:T(8,128)} async-done(((f32[1,2048,128]{1,2,0:T(8,128)}), f32[1,2048,128]{1,2,0:T(8,128)}) %all-reduce.23.cloned.1.call-update) | async-done | bytes 1048592 | tf_op jit(solution)/shard_map/psum | solution.py:18
  452.5 11.7 custom-call.56
  483.9 82.4 %all-reduce.25.cloned.1.call-done = f32[1,2048,128]{1,2,0:T(8,128)} async-done(((f32[1,2048,128]{1,2,0:T(8,128)}), f32[1,2048,128]{1,2,0:T(8,128)}) %all-reduce.25.cloned.1.call-update) | async-done | bytes 1048592 | tf_op jit(solution)/shard_map/psum | solution.py:18
  568.1 11.7 custom-call.58
  599.9 82.9 %all-reduce.27.cloned.1.call-done = f32[1,2048,128]{1,2,0:T(8,128)} async-done(((f32[1,2048,128]{1,2,0:T(8,128)}), f32[1,2048,128]{1,2,0:T(8,128)}) %all-reduce.27.cloned.1.call-update) | async-done | bytes 1048592 | tf_op jit(solution)/shard_map/psum | solution.py:18
  684.5 11.7 custom-call.60
  715.0 82.7 %all-reduce.29.cloned.1.call-done = f32[1,2048,128]{1,2,0:T(8,128)} async-done(((f32[1,2048,128]{1,2,0:T(8,128)}), f32[1,2048,128]{1,2,0:T(8,128)}) %all-reduce.29.cloned.1.call-update) | async-done | bytes 1048592 | tf_op jit(solution)/shard_map/psum | solution.py:18
  799.4 11.7 custom-call.62
  828.1 84.6 %all-reduce.31.cloned.1.call-done = f32[1,2048,128]{1,2,0:T(8,128)} async-done(((f32[1,2048,128]{1,2,0:T(8,128)}), f32[1,2048,128]{1,2,0:T(8,128)}) %all-reduce.31.cloned.1.call-update) | async-done | bytes 1048592 | tf_op jit(solution)/shard_map/psum | solution.py:18
  914.5 11.7 custom-call.64
  941.4 74.2 %all-gather.3.cloned.1.call-done = f32[1,1024,8,128]{3,1,0,2:T(8,128)} async-done(((f32[1,1024,1,128]{3,1,0,2:T(8,128)}), f32[1,1024,8,128]{3,1,0,2:T(8,128)}) %all-gather.3.cloned.1.call-update) | async-done | bytes 4194320 | tf_op jit(solution)/shard_map/all_gather | solution.py:104
  1054.6 80.3 %all-reduce.33.cloned.1.call-done = f32[1,2048,128]{1,2,0:T(8,128)} async-done(((f32[1,2048,128]{1,2,0:T(8,128)}), f32[1,2048,128]{1,2,0:T(8,128)}) %all-reduce.33.cloned.1.call-update) | async-done | bytes 1048592 | tf_op jit(solution)/shard_map/psum | solution.py:18
  1146.1 11.7 custom-call.66
  1172.9 80.5 %all-reduce.35.cloned.1.call-done = f32[1,2048,128]{1,2,0:T(8,128)} async-done(((f32[1,2048,128]{1,2,0:T(8,128)}), f32[1,2048,128]{1,2,0:T(8,128)}) %all-reduce.35.cloned.1.call-update) | async-done | bytes 1048592 | tf_op jit(solution)/shard_map/psum | solution.py:18
  1264.8 11.7 custom-call.68
  1291.3 80.5 %all-reduce.37.cloned.1.call-done = f32[1,2048,128]{1,2,0:T(8,128)} async-done(((f32[1,2048,128]{1,2,0:T(8,128)}), f32[1,2048,128]{1,2,0:T(8,128)}) %all-reduce.37.cloned.1.call-update) | async-done | bytes 1048592 | tf_op jit(solution)/shard_map/psum | solution.py:18
  1382.9 11.7 custom-call.70
  1409.3 80.4 %all-reduce.39.cloned.1.call-done = f32[1,2048,128]{1,2,0:T(8,128)} async-done(((f32[1,2048,128]{1,2,0:T(8,128)}), f32[1,2048,128]{1,2,0:T(8,128)}) %all-reduce.39.cloned.1.call-update) | async-done | bytes 1048592 | tf_op jit(solution)/shard_map/psum | solution.py:18
  1501.2 11.7 custom-call.72
  1527.5 80.5 %all-reduce.41.cloned.1.call-done = f32[1,2048,128]{1,2,0:T(8,128)} async-done(((f32[1,2048,128]{1,2,0:T(8,128)}), f32[1,2048,128]{1,2,0:T(8,128)}) %all-reduce.41.cloned.1.call-update) | async-done | bytes 1048592 | tf_op jit(solution)/shard_map/psum | solution.py:18
  1619.2 11.7 custom-call.74
  1645.4 80.4 %all-reduce.43.cloned.1.call-done = f32[1,2048,128]{1,2,0:T(8,128)} async-done(((f32[1,2048,128]{1,2,0:T(8,128)}), f32[1,2048,128]{1,2,0:T(8,128)}) %all-reduce.43.cloned.1.call-update) | async-done | bytes 1048592 | tf_op jit(solution)/shard_map/psum | solution.py:18
  1737.3 11.7 custom-call.76
  1763.4 80.5 %all-reduce.45.cloned.1.call-done = f32[1,2048,128]{1,2,0:T(8,128)} async-done(((f32[1,2048,128]{1,2,0:T(8,128)}), f32[1,2048,128]{1,2,0:T(8,128)}) %all-reduce.45.cloned.1.call-update) | async-done | bytes 1048592 | tf_op jit(solution)/shard_map/psum | solution.py:18
  1855.3 11.7 custom-call.78
  1881.2 80.5 %all-reduce.47.cloned.1.call-done = f32[1,2048,128]{1,2,0:T(8,128)} async-done(((f32[1,2048,128]{1,2,0:T(8,128)}), f32[1,2048,128]{1,2,0:T(8,128)}) %all-reduce.47.cloned.1.call-update) | async-done | bytes 1048592 | tf_op jit(solution)/shard_map/psum | solution.py:18
  (337 shorter events, 396.5 us)
Async XLA Ops:
  7.2 95.7 %all-reduce.17.cloned.1.call-start = ((), (), s32[]{:S(2)}) async-start(), calls=%async_computation | async-start | bytes 2097152 | tf_op jit(solution)/shard_map/psum | solution.py:18
  16.6 202.9 %all-reduce.19.cloned.1.call-start = ((), (), s32[]{:S(2)}) async-start(), calls=%async_computation.1 | async-start | bytes 2097152 | tf_op jit(solution)/shard_map/psum | solution.py:18
  133.5 201.4 %all-reduce.21.cloned.1.call-start = ((), (), s32[]{:S(2)}) async-start(), calls=%async_computation.2 | async-start | bytes 2097152 | tf_op jit(solution)/shard_map/psum | solution.py:18
  248.9 101.1 %copy-start.5 = (f32[1,2048,1,128]{1,3,2,0:T(8,128)}, f32[1,2048,1,128]{1,3,2,0:T(8,128)S(1)}, u32[]{:S(2)}) copy-start(f32[1,2048,1,128]{1,3,2,0:T(8,128)S(1)} %get-tuple-element.78) | copy-start | bytes 3145732
  249.0 201.7 %all-reduce.23.cloned.1.call-start = ((), (), s32[]{:S(2)}) async-start(), calls=%async_computation.3 | async-start | bytes 2097152 | tf_op jit(solution)/shard_map/psum | solution.py:18
  359.9 2.1 copy-start.6
  364.7 201.6 %all-reduce.25.cloned.1.call-start = ((), (), s32[]{:S(2)}) async-start(), calls=%async_computation.4 | async-start | bytes 2097152 | tf_op jit(solution)/shard_map/psum | solution.py:18
  384.9 92.7 %copy-start.1 = (f32[1,2048,1,128]{1,3,2,0:T(8,128)S(1)}, f32[1,2048,1,128]{1,3,2,0:T(8,128)}, u32[]{:S(2)}) copy-start(f32[1,2048,1,128]{1,3,2,0:T(8,128)} %get-tuple-element.76) | copy-start | bytes 3145732
  480.2 202.5 %all-reduce.27.cloned.1.call-start = ((), (), s32[]{:S(2)}) async-start(), calls=%async_computation.5 | async-start | bytes 2097152 | tf_op jit(solution)/shard_map/psum | solution.py:18
  596.8 200.9 %all-reduce.29.cloned.1.call-start = ((), (), s32[]{:S(2)}) async-start(), calls=%async_computation.6 | async-start | bytes 2097152 | tf_op jit(solution)/shard_map/psum | solution.py:18
  711.6 201.1 %all-reduce.31.cloned.1.call-start = ((), (), s32[]{:S(2)}) async-start(), calls=%async_computation.7 | async-start | bytes 2097152 | tf_op jit(solution)/shard_map/psum | solution.py:18
  826.7 188.8 %all-gather.3.cloned.1.call-start = ((), (), s32[]{:S(2)}) async-start(), calls=%async_computation.16 | async-start | bytes 4718592 | tf_op jit(solution)/shard_map/all_gather | solution.py:104
  941.3 85.3 %copy-start.7 = (s32[16,1,8]{0,2,1:T(8,128)S(1)}, s32[16,1,8]{0,2,1:T(8,128)}, u32[]{:S(2)}) copy-start(s32[16,1,8]{0,2,1:T(8,128)} %param.24) | copy-start | bytes 1540
  941.3 193.6 %all-reduce.33.cloned.1.call-start = ((), (), s32[]{:S(2)}) async-start(), calls=%async_computation.8 | async-start | bytes 2097152 | tf_op jit(solution)/shard_map/psum | solution.py:18
  1020.9 16.3 collective-permute-start
  1051.3 2.0 copy-start.8
  1054.6 198.8 %all-reduce.35.cloned.1.call-start = ((), (), s32[]{:S(2)}) async-start(), calls=%async_computation.9 | async-start | bytes 2097152 | tf_op jit(solution)/shard_map/psum | solution.py:18
  1134.9 9.7 collective-permute-start.1
  1172.8 199.0 %all-reduce.37.cloned.1.call-start = ((), (), s32[]{:S(2)}) async-start(), calls=%async_computation.10 | async-start | bytes 2097152 | tf_op jit(solution)/shard_map/psum | solution.py:18
  1253.3 10.0 collective-permute-start.2
  1291.3 198.5 %all-reduce.39.cloned.1.call-start = ((), (), s32[]{:S(2)}) async-start(), calls=%async_computation.11 | async-start | bytes 2097152 | tf_op jit(solution)/shard_map/psum | solution.py:18
  1371.8 9.6 collective-permute-start.3
  1409.3 198.7 %all-reduce.41.cloned.1.call-start = ((), (), s32[]{:S(2)}) async-start(), calls=%async_computation.12 | async-start | bytes 2097152 | tf_op jit(solution)/shard_map/psum | solution.py:18
  1489.7 10.0 collective-permute-start.4
  1527.4 198.4 %all-reduce.43.cloned.1.call-start = ((), (), s32[]{:S(2)}) async-start(), calls=%async_computation.13 | async-start | bytes 2097152 | tf_op jit(solution)/shard_map/psum | solution.py:18
  1608.0 9.8 collective-permute-start.5
  1645.4 198.5 %all-reduce.45.cloned.1.call-start = ((), (), s32[]{:S(2)}) async-start(), calls=%async_computation.14 | async-start | bytes 2097152 | tf_op jit(solution)/shard_map/psum | solution.py:18
  1725.8 10.0 collective-permute-start.6
  1763.4 198.3 %all-reduce.47.cloned.1.call-start = ((), (), s32[]{:S(2)}) async-start(), calls=%async_computation.15 | async-start | bytes 2097152 | tf_op jit(solution)/shard_map/psum | solution.py:18
  1843.9 9.9 collective-permute-start.7
  1879.9 91.6 %copy-start.2 = (f32[1,2048,1,128]{1,3,2,0:T(8,128)S(1)}, f32[1,2048,1,128]{1,3,2,0:T(8,128)}, u32[]{:S(2)}) copy-start(f32[1,2048,1,128]{1,3,2,0:T(8,128)} %get-tuple-element.68) | copy-start | bytes 3145732
  1961.7 12.7 collective-permute-start.8
  (3 other events, 4.0 us)
Sparse Core Ops, SparseCore 0:
  16.7 86.0 all-reduce.16
  133.6 85.8 all-reduce.18
  249.1 85.8 all-reduce.20
  364.8 85.8 all-reduce.22
  480.3 85.8 all-reduce.24
  596.9 85.8 all-reduce.26
  711.8 85.8 all-reduce.28
  826.9 85.8 all-reduce.30
  941.4 74.1 all-gather.2
  1054.7 80.1 all-reduce.32
  1172.9 80.3 all-reduce.34
  1291.4 80.3 all-reduce.36
  1409.4 80.3 all-reduce.38
  1527.6 80.3 all-reduce.40
  1645.5 80.3 all-reduce.42
  1763.5 80.3 all-reduce.44
  1881.3 80.3 all-reduce.46
where the time goes:
time: 2020 us; the launch traced here: 2010 us
  waiting for transfers between devices  1370 us (68%)
  other arithmetic  413 us (20%)
  between operations  69.7 us (3%)
  matrix products  69.2 us (3%)
  starting transfers between devices  51 us (3%)
  local copies, waits for them, and re-layouts  38.3 us (2%)
    psum x16, waiting for transfers between devices, broadcast(): return lax.psum(jnp.where(mine, value, jnp.zeros_like(value)), axis)  1290 us
    another operation x48, other arithmetic, panel_factor(): lower_part = jnp.linalg.cholesky(column_tail[:, :NB])  199 us
    another operation x32, other arithmetic, panel_factor(): lax.linalg.triangular_solve(lower_part, column_tail[:, NB:], left_side=Fa...  168 us
    all_gather x1, waiting for transfers between devices, body(): lax.all_gather(contrib[:, :, :, None, :], 'grid', axis=3, tiled=True)  74.2 us
    ppermute x9, starting transfers between devices, swapped_2(): return lax.ppermute(value, axis, pairs)  48.5 us
  transfers between devices with their start and end apart: 26, of which 17 were waited for; matrix products, arithmetic and copies ran while one was open for 2% of the time, Pallas kernels for 0%

commit v1 on v0

--- a/solution.py
+++ b/solution.py
@@ -2,6 +2,7 @@
 import jax.numpy as jnp
 from jax import lax
 from jax.sharding import PartitionSpec as P
+from jax.lax import all_gather
 
 F = 2048
 PIVOTS = 1024
@@ -15,7 +16,8 @@
 
 def broadcast(value, axis, root):
     mine = lax.axis_index(axis) == root
-    return lax.psum(jnp.where(mine, value, jnp.zeros_like(value)), axis)
+    squares_form = lambda v0, axis_id: all_gather(v0, axis_id).sum(axis=0)
+    return squares_form(jnp.where(mine, value, jnp.zeros_like(value)), axis)
 
 
 def swapped_2(value, axis, distance):

time: 2020 us -> 2540 us (1.26)
  waiting for transfers between devices: 1370 us -> 1700 us
  local copies, waits for them, and re-layouts: 38.3 us -> 143 us
  other arithmetic: 413 us -> 511 us
  starting transfers between devices: 51 us -> 14.2 us
    all_gather x0 -> x16, waiting for transfers between devices: none -> 1630 us  [broadcast(): squares_form = lambda v0, axis_id: all_gather(v0, axis_id).sum(axis=0)]
    psum x16 -> x0, waiting for transfers between devices: 1290 us -> none  [broadcast(): return lax.psum(jnp.where(mine, value, jnp.zeros_like(value)), axis)]
    reduce_sum x0 -> x16, other arithmetic: none -> 64.6 us  [broadcast(): squares_form = lambda v0, axis_id: all_gather(v0, axis_id).sum(axis=0)]
    ppermute x9, starting transfers between devices: 48.5 us -> 11.8 us  [swapped_2(): return lax.ppermute(value, axis, pairs)]
    unnamed x21 -> x109, local copies, waits for them, and re-layouts: 11.2 us -> 41.9 us
    select_n x0 -> x14, local copies, waits for them, and re-layouts: none -> 28.1 us  [broadcast(): return squares_form(jnp.where(mine, value, jnp.zeros_like(value)), axis)]
where the time goes in v1:
time: 2540 us; the launch traced here: 2520 us
  waiting for transfers between devices  1700 us (67%)
  other arithmetic  511 us (20%)
  local copies, waits for them, and re-layouts  143 us (6%)
  matrix products  87.6 us (3%)
  between operations  69.6 us (3%)
    all_gather x16, waiting for transfers between devices, broadcast(): squares_form = lambda v0, axis_id: all_gather(v0, axis_id).sum(axis=0)  1630 us
    another operation x48, other arithmetic, panel_factor(): lower_part = jnp.linalg.cholesky(column_tail[:, :NB])  206 us
    another operation x32, other arithmetic, panel_factor(): lax.linalg.triangular_solve(lower_part, column_tail[:, NB:], left_side=Fa...  179 us
    all_gather x1, waiting for transfers between devices, body(): lax.all_gather(contrib[:, :, :, None, :], 'grid', axis=3, tiled=True)  69.4 us
    reduce_sum x16, other arithmetic, broadcast(): squares_form = lambda v0, axis_id: all_gather(v0, axis_id).sum(axis=0)  64.6 us
  transfers between devices with their start and end apart: 26, of which 17 were waited for; matrix products, arithmetic and copies ran while one was open for 2% of the time, Pallas kernels for 0%

profile of v1, /device:TPU:1, one launch (start us, length us, event | category | flops | bytes accessed | tf_op | source)
XLA Modules:
  0.0 2522.6 jit_solution(5092807209873915012)
XLA Ops:
  23.5 107.6 %all-gather.48.cloned.1.call-done = f32[8,2048,1,128]{3,1,2,0:T(8,128)} async-done(((f32[1,2048,1,128]{3,1,2,0:T(8,128)}), f32[8,2048,1,128]{3,1,2,0:T(8,128)}) %all-gather.48.cloned.1.call-update) | async-done | bytes 8388624 | tf_op jit(solution)/shard_map/all_gather | solution.py:19
  140.3 11.7 custom-call.50
  170.5 102.8 %all-gather.50.cloned.1.call-done = f32[16384,128]{0,1:T(8,128)} async-done(((f32[2048,128]{0,1:T(8,128)}), f32[16384,128]{0,1:T(8,128)}) %all-gather.50.cloned.1.call-update) | async-done | bytes 8388624 | tf_op jit(solution)/shard_map/all_gather | solution.py:19
  285.5 11.9 custom-call.52
  318.1 102.8 %all-gather.22.cloned.1.call-done = f32[8,1,2048,128]{3,2,1,0:T(8,128)} async-done(((f32[1,1,2048,128]{3,2,1,0:T(8,128)}), f32[8,1,2048,128]{3,2,1,0:T(8,128)}) %all-gather.22.cloned.1.call-update) | async-done | bytes 8388624 | tf_op jit(solution)/shard_map/all_gather | solution.py:19
  427.8 11.7 custom-call.54
  464.5 100.4 %all-gather.24.cloned.1.call-done = f32[8,1,2048,128]{3,2,1,0:T(8,128)} async-done(((f32[1,1,2048,128]{3,2,1,0:T(8,128)}), f32[8,1,2048,128]{3,2,1,0:T(8,128)}) %all-gather.24.cloned.1.call-update) | async-done | bytes 8388624 | tf_op jit(solution)/shard_map/all_gather | solution.py:19
  574.1 11.7 custom-call.56
  614.8 100.5 %all-gather.26.cloned.1.call-done = f32[8,1,2048,128]{3,2,1,0:T(8,128)} async-done(((f32[1,1,2048,128]{3,2,1,0:T(8,128)}), f32[8,1,2048,128]{3,2,1,0:T(8,128)}) %all-gather.26.cloned.1.call-update) | async-done | bytes 8388624 | tf_op jit(solution)/shard_map/all_gather | solution.py:19
  727.3 13.2 custom-call.58
  774.1 100.5 %all-gather.28.cloned.1.call-done = f32[8,1,2048,128]{3,2,1,0:T(8,128)} async-done(((f32[1,1,2048,128]{3,2,1,0:T(8,128)}), f32[8,1,2048,128]{3,2,1,0:T(8,128)}) %all-gather.28.cloned.1.call-update) | async-done | bytes 8388624 | tf_op jit(solution)/shard_map/all_gather | solution.py:19
  886.6 13.2 custom-call.60
  933.5 100.2 %all-gather.30.cloned.1.call-done = f32[8,1,2048,128]{3,2,1,0:T(8,128)} async-done(((f32[1,1,2048,128]{3,2,1,0:T(8,128)}), f32[8,1,2048,128]{3,2,1,0:T(8,128)}) %all-gather.30.cloned.1.call-update) | async-done | bytes 8388624 | tf_op jit(solution)/shard_map/all_gather | solution.py:19
  1045.7 13.2 custom-call.62
  1109.4 83.1 %all-gather.32.cloned.1.call-done = f32[8,1,2048,128]{3,2,1,0:T(8,128)} async-done(((f32[1,1,2048,128]{3,2,1,0:T(8,128)}), f32[8,1,2048,128]{3,2,1,0:T(8,128)}) %all-gather.32.cloned.1.call-update) | async-done | bytes 8388624 | tf_op jit(solution)/shard_map/all_gather | solution.py:19
  1196.9 11.9 custom-call.64
  1222.8 69.4 %all-gather.52.cloned.1.call-done = f32[1,1024,8,128]{3,1,0,2:T(8,128)} async-done(((f32[1,1024,1,128]{3,1,0,2:T(8,128)}), f32[1,1024,8,128]{3,1,0,2:T(8,128)}) %all-gather.52.cloned.1.call-update) | async-done | bytes 4194320 | tf_op jit(solution)/shard_map/all_gather | solution.py:106
  1335.6 104.2 %all-gather.34.cloned.1.call-done = f32[8,1,2048,128]{3,2,1,0:T(8,128)} async-done(((f32[1,1,2048,128]{3,2,1,0:T(8,128)}), f32[8,1,2048,128]{3,2,1,0:T(8,128)}) %all-gather.34.cloned.1.call-update) | async-done | bytes 8388624 | tf_op jit(solution)/shard_map/all_gather | solution.py:19
  1455.4 11.7 custom-call.66
  1483.8 104.3 %all-gather.54.cloned.1.call-done = f32[16384,128]{0,1:T(8,128)} async-done(((f32[2048,128]{0,1:T(8,128)}), f32[16384,128]{0,1:T(8,128)}) %all-gather.54.cloned.1.call-update) | async-done | bytes 8388624 | tf_op jit(solution)/shard_map/all_gather | solution.py:19
  1609.1 11.7 custom-call.68
  1639.9 104.1 %all-gather.36.cloned.1.call-done = f32[8,1,2048,128]{3,2,1,0:T(8,128)} async-done(((f32[1,1,2048,128]{3,2,1,0:T(8,128)}), f32[8,1,2048,128]{3,2,1,0:T(8,128)}) %all-gather.36.cloned.1.call-update) | async-done | bytes 8388624 | tf_op jit(solution)/shard_map/all_gather | solution.py:19
  1756.8 11.7 custom-call.70
  1787.9 104.2 %all-gather.38.cloned.1.call-done = f32[8,1,2048,128]{3,2,1,0:T(8,128)} async-done(((f32[1,1,2048,128]{3,2,1,0:T(8,128)}), f32[8,1,2048,128]{3,2,1,0:T(8,128)}) %all-gather.38.cloned.1.call-update) | async-done | bytes 8388624 | tf_op jit(solution)/shard_map/all_gather | solution.py:19
  1904.7 11.7 custom-call.72
  1933.0 104.5 %all-gather.40.cloned.1.call-done = f32[8,1,2048,128]{3,2,1,0:T(8,128)} async-done(((f32[1,1,2048,128]{3,2,1,0:T(8,128)}), f32[8,1,2048,128]{3,2,1,0:T(8,128)}) %all-gather.40.cloned.1.call-update) | async-done | bytes 8388624 | tf_op jit(solution)/shard_map/all_gather | solution.py:19
  2050.4 11.7 custom-call.74
  2079.2 104.4 %all-gather.42.cloned.1.call-done = f32[8,1,2048,128]{3,2,1,0:T(8,128)} async-done(((f32[1,1,2048,128]{3,2,1,0:T(8,128)}), f32[8,1,2048,128]{3,2,1,0:T(8,128)}) %all-gather.42.cloned.1.call-update) | async-done | bytes 8388624 | tf_op jit(solution)/shard_map/all_gather | solution.py:19
  2196.2 11.7 custom-call.76
  2223.6 104.2 %all-gather.44.cloned.1.call-done = f32[8,1,2048,128]{3,2,1,0:T(8,128)} async-done(((f32[1,1,2048,128]{3,2,1,0:T(8,128)}), f32[8,1,2048,128]{3,2,1,0:T(8,128)}) %all-gather.44.cloned.1.call-update) | async-done | bytes 8388624 | tf_op jit(solution)/shard_map/all_gather | solution.py:19
  2340.6 11.7 custom-call.78
  2374.6 99.7 %all-gather.46.cloned.1.call-done = f32[8,1,2048,128]{3,2,1,0:T(8,128)} async-done(((f32[1,1,2048,128]{3,2,1,0:T(8,128)}), f32[8,1,2048,128]{3,2,1,0:T(8,128)}) %all-gather.46.cloned.1.call-update) | async-done | bytes 8388624 | tf_op jit(solution)/shard_map/all_gather | solution.py:19
  (479 shorter events, 575.8 us)
Async XLA Ops:
  7.2 124.0 %all-gather.48.cloned.1.call-start = ((), (), s32[]{:S(2)}) async-start(), calls=%async_computation.13 | async-start | bytes 9437184 | tf_op jit(solution)/shard_map/all_gather | solution.py:19
  17.2 148.4 %copy-start.3 = (f32[1,2048,2,128]{1,3,2,0:T(8,128)}, f32[1,2048,2,128]{1,3,2,0:T(8,128)S(1)}, u32[]{:S(2)}) copy-start(f32[1,2048,2,128]{1,3,2,0:T(8,128)S(1)} %fusion.61) | copy-start | bytes 6291460
  20.9 252.4 %all-gather.50.cloned.1.call-start = ((), (), s32[]{:S(2)}) async-start(), calls=%async_computation.14 | async-start | bytes 9437184 | tf_op jit(solution)/shard_map/all_gather | solution.py:19
  165.5 117.7 %copy-start.23 = (f32[1,128,128]{1,2,0:T(8,128)}, f32[1,128,128]{1,2,0:T(8,128)S(1)}, u32[]{:S(2)}) copy-start(f32[1,128,128]{1,2,0:T(8,128)S(1)} %copy.274) | copy-start | bytes 196612
  165.6 117.6 %copy-start.37 = (f32[128,128]{0,1:T(8,128)}, f32[128,128]{0,1:T(8,128)S(1)}, u32[]{:S(2)}) copy-start(f32[128,128]{0,1:T(8,128)S(1)} %copy.273) | copy-start | bytes 196612
  168.2 252.7 %all-gather.22.cloned.1.call-start = ((), (), s32[]{:S(2)}) async-start(), calls=%async_computation | async-start | bytes 9437184 | tf_op jit(solution)/shard_map/all_gather | solution.py:19
  315.7 249.3 %all-gather.24.cloned.1.call-start = ((), (), s32[]{:S(2)}) async-start(), calls=%async_computation.1 | async-start | bytes 9437184 | tf_op jit(solution)/shard_map/all_gather | solution.py:19
  459.8 255.6 %all-gather.26.cloned.1.call-start = ((), (), s32[]{:S(2)}) async-start(), calls=%async_computation.2 | async-start | bytes 9437184 | tf_op jit(solution)/shard_map/all_gather | solution.py:19
  610.2 264.4 %all-gather.28.cloned.1.call-start = ((), (), s32[]{:S(2)}) async-start(), calls=%async_computation.3 | async-start | bytes 9437184 | tf_op jit(solution)/shard_map/all_gather | solution.py:19
  769.4 264.3 %all-gather.30.cloned.1.call-start = ((), (), s32[]{:S(2)}) async-start(), calls=%async_computation.4 | async-start | bytes 9437184 | tf_op jit(solution)/shard_map/all_gather | solution.py:19
  928.6 263.9 %all-gather.32.cloned.1.call-start = ((), (), s32[]{:S(2)}) async-start(), calls=%async_computation.5 | async-start | bytes 9437184 | tf_op jit(solution)/shard_map/all_gather | solution.py:19
  1087.3 204.9 %all-gather.52.cloned.1.call-start = ((), (), s32[]{:S(2)}) async-start(), calls=%async_computation.15 | async-start | bytes 4718592 | tf_op jit(solution)/shard_map/all_gather | solution.py:106
  1222.7 217.1 %all-gather.34.cloned.1.call-start = ((), (), s32[]{:S(2)}) async-start(), calls=%async_computation.6 | async-start | bytes 9437184 | tf_op jit(solution)/shard_map/all_gather | solution.py:19
  1297.5 16.1 collective-permute-start
  1335.6 252.5 %all-gather.54.cloned.1.call-start = ((), (), s32[]{:S(2)}) async-start(), calls=%async_computation.16 | async-start | bytes 9437184 | tf_op jit(solution)/shard_map/all_gather | solution.py:19
  1447.2 4.9 collective-permute-start.1
  1483.6 260.4 %all-gather.36.cloned.1.call-start = ((), (), s32[]{:S(2)}) async-start(), calls=%async_computation.7 | async-start | bytes 9437184 | tf_op jit(solution)/shard_map/all_gather | solution.py:19
  1600.1 5.7 collective-permute-start.2
  1639.8 252.2 %all-gather.38.cloned.1.call-start = ((), (), s32[]{:S(2)}) async-start(), calls=%async_computation.8 | async-start | bytes 9437184 | tf_op jit(solution)/shard_map/all_gather | solution.py:19
  1749.2 5.8 collective-permute-start.3
  1787.8 114.5 %copy-start.48 = (f32[1,256,128]{1,2,0:T(8,128)S(1)}, f32[1,256,128]{1,2,0:T(8,128)}, u32[]{:S(2)}) copy-start(f32[1,256,128]{1,2,0:T(8,128)} %get-tuple-element.65) | copy-start | bytes 393220
  1787.8 249.7 %all-gather.40.cloned.1.call-start = ((), (), s32[]{:S(2)}) async-start(), calls=%async_computation.9 | async-start | bytes 9437184 | tf_op jit(solution)/shard_map/all_gather | solution.py:19
  1897.2 5.9 collective-permute-start.4
  1932.9 115.1 %copy-start.35 = (f32[1,384,128]{1,2,0:T(8,128)S(1)}, f32[1,384,128]{1,2,0:T(8,128)}, u32[]{:S(2)}) copy-start(f32[1,384,128]{1,2,0:T(8,128)} %get-tuple-element.63) | copy-start | bytes 589828
  1932.9 250.6 %all-gather.42.cloned.1.call-start = ((), (), s32[]{:S(2)}) async-start(), calls=%async_computation.10 | async-start | bytes 9437184 | tf_op jit(solution)/shard_map/all_gather | solution.py:19
  2042.7 6.2 collective-permute-start.5
  2079.1 248.6 %all-gather.44.cloned.1.call-start = ((), (), s32[]{:S(2)}) async-start(), calls=%async_computation.11 | async-start | bytes 9437184 | tf_op jit(solution)/shard_map/all_gather | solution.py:19
  2188.7 5.6 collective-permute-start.6
  2223.5 114.5 %copy-start.33 = (f32[1,640,128]{1,2,0:T(8,128)S(1)}, f32[1,640,128]{1,2,0:T(8,128)}, u32[]{:S(2)}) copy-start(f32[1,640,128]{1,2,0:T(8,128)} %get-tuple-element.59) | copy-start | bytes 983044
  2223.5 250.8 %all-gather.46.cloned.1.call-start = ((), (), s32[]{:S(2)}) async-start(), calls=%async_computation.12 | async-start | bytes 9437184 | tf_op jit(solution)/shard_map/all_gather | solution.py:19
  2333.0 6.1 collective-permute-start.7
  2478.5 7.4 collective-permute-start.8
  (46 other events, 593.1 us)
Sparse Core Ops, SparseCore 0:
  21.0 110.0 all-gather.47
  168.3 105.0 all-gather.49
  315.8 105.0 all-gather.21
  459.9 104.9 all-gather.23
  610.3 104.9 all-gather.25
  769.5 105.0 all-gather.27
  928.7 104.9 all-gather.29
  1087.4 104.9 all-gather.31
  1222.8 69.3 all-gather.51
  1335.7 104.0 all-gather.33
  1483.7 104.4 all-gather.53
  1639.9 103.9 all-gather.35
  1787.9 104.0 all-gather.37
  1933.0 104.4 all-gather.39
  2079.2 104.2 all-gather.41
  2223.6 104.0 all-gather.43
  2370.0 104.2 all-gather.45
